TPU v7x, 512 devices: a whole 4x4x16 slice. The times are simulated.
512 devices in a mesh: grp: 32 (over y, z_lo), tp: 16 (over z_hi, x, core).
Axes of the slice: x: 4, y: 4, z: 16 (z_hi: 2, z_lo: 8; z = z_hi * 8 + z_lo), core: 2. Of those that a mesh axis runs over, the one named last changes fastest.
Arguments:
- tokens: bfloat16 [65536, 1536], P(('grp', 'tp')), may hold values from -6 to 6
- attn_gain: float32 [1536], replicated, may hold values from 0.1 to 1.9
- ffn_gain: float32 [1536], replicated, may hold values from 0.1 to 1.9
- w_query: bfloat16 [1536, 1024], P(None, 'tp')
- key_value_weight: bfloat16 [1536, 1024], P(None, 'tp'), may hold values from -0.15625 to 0.15625
- w_out: bfloat16 [1024, 1536], P('tp'), may hold values from -0.1875 to 0.1875
- segment_ids: int32 [65536], P(('grp', 'tp')), may hold values from 0 to 65535, as said below
- expert_ids: int32 [65536, 2], P(('grp', 'tp')), may hold values from 0 to 7, all different within a row; in each aligned block of 128 rows (0 to 127, 128 to 255, ...) at most 48 rows name the same one
- route_weights: float32 [65536, 2], P(('grp', 'tp')), may hold values from 0.2 to 1
- w_gate: bfloat16 [1536, 4096], P(None, 'tp'), may hold values from -0.15625 to 0.15625
- w_up: bfloat16 [1536, 4096], P(None, 'tp'), may hold values from -0.15625 to 0.15625
- w_down: bfloat16 [4096, 1536], P('tp'), may hold values from -0.25 to 0.25
- page_table: int32 [32, 128], P('grp'), may hold values from 0 to 127, each once within a row
Outputs:
- hidden_out: bfloat16 [65536, 1536], P(('grp', 'tp'))
- kv_cache: bfloat16 [4096, 16, 1024], P(('grp', 'tp'))
Inputs may be any that keep to these rules, and one draw needn't show every extreme that they name: `segment_ids`: each token's number is the stream position of its prompt's first token, so numbers never fall along the stream; a prompt covers at most 1024 tokens and some prompt exactly 1024; a prompt runs from every group into the next; the last token of the stream is a prompt of its own. `expert_ids`: in the tokens of one device no expert is named more than 48 times; in some device's tokens one expert is named exactly 48 times. `page_table`: each row names every page of the group once.
All inputs are finite; a program needn't handle non-finite values.
Results may differ from a plain program's by a relative error of at most 0.015.
The roundings to bfloat16 on the way count: a program that leaves them out, or rounds other values in their place, can miss the bound.
Values may be sent and summed in bfloat16 or wider, within the bound.
No kernel may reach another device: no remote copies, remote signals or barrier semaphores. Data moves between devices by JAX's collectives and lax.ppermute only.
A program may use at most 64 MiB of HBM per device.

v0:
```python
import jax
import jax.numpy as jnp
from jax import lax
from jax.sharding import PartitionSpec as P

HEAD_SIZE = 64
PAGE = 16


def partner_2(block, axis, bit):
    count = lax.axis_size(axis)
    route = []
    for low in range(count):
        high = low | 1 << bit
        if high != low and high < count:
            route += [(low, high), (high, low)]
    return lax.ppermute(block, axis, route)


def from_behind(block, axis, distance):
    devices = range(lax.axis_size(axis))
    route = [(i - distance, i) for i in devices if i - distance in devices]
    return lax.ppermute(block, axis, route)


def rms_scale(row_data, gain_vec):
    values = row_data.astype(jnp.float32)
    inverse = lax.rsqrt(jnp.mean(values * values, axis=-1, keepdims=True) + 1e-05)
    return (values * inverse * gain_vec).astype(jnp.bfloat16)


def attend_blocks(query_rows, key_cat, value_cat, seg_query, seg_cat, maxlen, offset, block_rows):
    group_tok = query_rows.shape[0]
    key_span = maxlen + block_rows

    def one_block(block_index):
        first_row = block_index * block_rows
        query_block = lax.dynamic_slice_in_dim(query_rows, first_row, block_rows, 0)
        seg_block = lax.dynamic_slice_in_dim(seg_query, first_row, block_rows, 0)
        key_block = lax.dynamic_slice_in_dim(key_cat, first_row + offset, key_span, 0)
        value_block = lax.dynamic_slice_in_dim(value_cat, first_row + offset, key_span, 0)
        seg_keys = lax.dynamic_slice_in_dim(seg_cat, first_row + offset, key_span, 0)
        key_pos = first_row - maxlen + jnp.arange(key_span, dtype=jnp.int32)
        query_pos = first_row + jnp.arange(block_rows, dtype=jnp.int32)
        scores = (
            jnp.einsum("qhd,khd->hqk", query_block, key_block, preferred_element_type=jnp.float32)
            * 0.125
        )
        allowed = (seg_block[:, None] == seg_keys[None, :]) & (
            key_pos[None, :] <= query_pos[:, None]
        )
        scores = jnp.where(allowed[None], scores, -1e30)
        row_max = jnp.max(scores, axis=-1, keepdims=True)
        exponent = jnp.exp(scores - row_max)
        attention = (exponent / jnp.sum(exponent, axis=-1, keepdims=True)).astype(jnp.bfloat16)
        result = jnp.einsum(
            "hqk,khd->qhd", attention, value_block, preferred_element_type=jnp.float32
        )
        return result.astype(jnp.bfloat16)

    blocks = lax.map(one_block, jnp.arange(group_tok // block_rows, dtype=jnp.int32))
    return blocks.reshape(group_tok, -1)


def body(
    tokens,
    attn_gain,
    ffn_gain,
    w_query,
    key_value_weight,
    w_out,
    segment_ids,
    expert_ids,
    route_weights,
    w_gate,
    w_up,
    w_down,
    page_table,
):
    tok_rows = tokens.shape[0]
    tp_size = lax.axis_size("tp")
    head_cols = w_query.shape[1]
    heads_here = head_cols // HEAD_SIZE
    normed_in = rms_scale(tokens, attn_gain)
    both_cols = jnp.concatenate([w_query, key_value_weight], axis=1)
    projected = jnp.dot(
        lax.all_gather(normed_in, "tp", axis=0, tiled=True),
        both_cols,
        preferred_element_type=jnp.float32,
    ).astype(jnp.bfloat16)
    group_tok = projected.shape[0]
    query_rows = projected[:, :head_cols].reshape(group_tok, heads_here, HEAD_SIZE)
    own_slice = projected[:, head_cols:]
    page_count = group_tok // PAGE
    page_order = page_table[0]
    page_ids = jnp.arange(page_count, dtype=jnp.int32)
    source_block = jnp.sum(
        jnp.where(page_order[None, :] == page_ids[:, None], page_ids[None, :], 0), axis=1
    )
    ordered_pages = own_slice.reshape(page_count, PAGE, head_cols)[source_block]
    kv_cache = lax.all_to_all(ordered_pages, "tp", split_axis=0, concat_axis=2, tiled=True)
    seg_all = lax.all_gather(segment_ids, "tp", axis=0, tiled=True)
    maxlen = group_tok // 2
    block_rows = min(512, group_tok)
    low_half = lax.axis_index("tp") < tp_size // 2
    pair_bit = tp_size.bit_length() - 2
    partner = partner_2(own_slice, "tp", pair_bit)
    key_rows = jnp.where(low_half, own_slice, partner)
    value_rows = jnp.where(low_half, partner, own_slice)
    tail_keys, tail_values, tail_seg = from_behind((key_rows, value_rows, seg_all), "grp", 1)
    tail_seg = jnp.where(lax.axis_index("grp") > 0, tail_seg, -1)
    key_cat = jnp.concatenate([tail_keys, key_rows], 0).reshape(-1, heads_here, HEAD_SIZE)
    value_cat = jnp.concatenate([tail_values, value_rows], 0).reshape(-1, heads_here, HEAD_SIZE)
    seg_cat = jnp.concatenate([tail_seg, seg_all], 0)
    attended = attend_blocks(
        query_rows, key_cat, value_cat, seg_all, seg_cat, maxlen, group_tok - maxlen, block_rows
    )
    token_heads = lax.all_to_all(attended, "tp", split_axis=0, concat_axis=1, tiled=True)
    out_sum = jnp.dot(
        token_heads,
        lax.all_gather(w_out, "tp", axis=0, tiled=True),
        preferred_element_type=jnp.float32,
    )
    mid_state = (tokens.astype(jnp.float32) + out_sum).astype(jnp.bfloat16)
    normed_mid = rms_scale(mid_state, ffn_gain)
    expert_count = tp_size // 2
    choice_count = expert_ids.shape[1]
    capacity = min(tok_rows, 3 * tok_rows * choice_count // (2 * expert_count))
    routes_flat = expert_ids.reshape(-1)
    onehot = (routes_flat[:, None] == jnp.arange(expert_count, dtype=jnp.int32)[None, :]).astype(
        jnp.int32
    )
    earlier = jnp.cumsum(onehot, axis=0) - onehot
    slot_index = jnp.sum(earlier * onehot, axis=-1)
    target_slot = routes_flat * capacity + slot_index
    placement_map = (
        target_slot[:, None] == jnp.arange(expert_count * capacity, dtype=jnp.int32)[None, :]
    )
    placement_map = placement_map.reshape(tok_rows, choice_count, expert_count * capacity)
    select_map = jnp.sum(placement_map.astype(jnp.int32), axis=1).astype(jnp.bfloat16)
    model_width = normed_mid.shape[1]
    buffers = jnp.einsum(
        "te,td->ed", select_map, normed_mid, preferred_element_type=jnp.float32
    ).astype(jnp.bfloat16)
    send_buf = jnp.broadcast_to(
        buffers.reshape(expert_count, 1, capacity, model_width),
        (expert_count, 2, capacity, model_width),
    )
    send_buf = send_buf.reshape(2 * expert_count, capacity, model_width)
    row_data = lax.all_to_all(send_buf, "tp", split_axis=0, concat_axis=0, tiled=True)
    slot_count = row_data.shape[1]
    flat_rows = row_data.reshape(-1, model_width)
    gate_act = jnp.dot(flat_rows, w_gate, preferred_element_type=jnp.float32)
    up_act = jnp.dot(flat_rows, w_up, preferred_element_type=jnp.float32)
    activated = (jax.nn.silu(gate_act) * up_act).astype(jnp.bfloat16)
    half_out = jnp.dot(activated, w_down, preferred_element_type=jnp.float32).astype(jnp.bfloat16)
    half_out = half_out.reshape(row_data.shape[0], slot_count, model_width)
    returned = lax.all_to_all(half_out, "tp", split_axis=0, concat_axis=0, tiled=True)
    halves = returned.reshape(expert_count, 2, capacity, model_width)
    summed = (halves[:, 0].astype(jnp.float32) + halves[:, 1].astype(jnp.float32)).reshape(
        expert_count * capacity, model_width
    )
    picked = summed[target_slot].reshape(tok_rows, choice_count, model_width)
    expert_sum = jnp.sum(picked * route_weights[..., None], axis=1)
    hidden_out = (mid_state.astype(jnp.float32) + expert_sum).astype(jnp.bfloat16)
    return (hidden_out, kv_cache)


def solution(mesh):
    in_specs = (
        P(("grp", "tp"), None),
        P(),
        P(),
        P(None, "tp"),
        P(None, "tp"),
        P("tp", None),
        P(("grp", "tp")),
        P(("grp", "tp"), None),
        P(("grp", "tp"), None),
        P(None, "tp"),
        P(None, "tp"),
        P("tp", None),
        P("grp", None),
    )
    out_specs = (P(("grp", "tp"), None), P(("grp", "tp"), None, None))
    return jax.shard_map(body, mesh=mesh, in_specs=in_specs, out_specs=out_specs, check_vma=False)
```

profile of v0, /device:TPU:103, one launch (start us, length us, event | category | flops | bytes accessed | tf_op | source)
XLA Modules:
  0.0 620.0 jit_solution(16437475761888153532)
XLA Ops:
  10.4 152.5 %all-gather.4.cloned.1.call-done = bf16[2048,1536]{1,0:T(8,128)(2,1)} async-done(((bf16[128,1536]{1,0:T(8,128)(2,1)}), bf16[2048,1536]{1,0:T(8,128)(2,1)}) %all-gather.4.cloned.1.call-update) | async-done | bytes 6291472 | tf_op jit(solution)/shard_map/all_gather | solution.py:87
  163.0 4.9 convolution_convert_fusion.2
  169.9 43.4 %all-gather = s32[16,1,128]{2,1,0:T(1,128)S(1)} all-gather(s32[1,1,128]{2,1,0:T(1,128)S(1)} %bitcast.102), channel_id=1, replica_groups=mesh['grp'=32,'tp'=16] {'tp'}, dimensions={0}, use_global_device_ids=true | all-gather | bytes 8704 | tf_op jit(solution)/shard_map/all_gather | solution.py:102
  217.2 3.0 collective-permute-done.2
  222.1 5.5 collective-permute-done.3
  227.7 5.6 collective-permute-done.1
  233.4 15.4 %while.12 = (s32[]{:T(128)}, bf16[4,512,1,64]{1,3,2,0:T(8,128)(2,1)S(1)}, s32[4]{0:T(128)S(1)}, bf16[4096,1,64]{0,2,1:T(8,128)(2,1)S(1)}, s32[2048]{0:T(1024)S(1...) while((s32[]{:T(128)}, ...), condition=%wide.region_4.5_spmd, body=%wide.region_1.4_spmd.sunk | while | flops 210011136 | bytes 10017057 | solution.py:61
  249.9 20.4 %all-to-all-start = ((bf16[16,128,64]{1,2,0:T(8,128)(2,1)}), bf16[16,128,64]{1,2,0:T(8,128)(2,1)S(1)}, u32[]{:S(2)}, u32[]{:S(2)}) async-start(bf16[16,128,64]{1,2,0:T(8,128)(2,1)} %copy.44), calls=%async_computation | async-start | bytes 524288 | tf_op jit(solution)/shard_map/all_to_all | solution.py:118
  271.9 55.3 %all-gather.6.cloned.1.call-done = bf16[1024,1536]{1,0:T(8,128)(2,1)} async-done(((bf16[64,1536]{1,0:T(8,128)(2,1)}), bf16[1024,1536]{1,0:T(8,128)(2,1)}) %all-gather.6.cloned.1.call-update) | async-done | bytes 3145744 | tf_op jit(solution)/shard_map/all_gather | solution.py:121
  327.2 2.6 multiply_reduce_fusion.1
  332.9 6.5 %all-to-all-start.1 = ((bf16[16,48,1536]{2,1,0:T(8,128)(2,1)}), bf16[16,48,1536]{2,1,0:T(8,128)(2,1)S(1)}, u32[]{:S(2)}, u32[]{:S(2)}) async-start(bf16[16,48,1536]{2,1,0:T(8,128)(2,1)} %bitcast.17), calls=%async_computation.1 | async-start | bytes 4718592 | tf_op jit(solution)/shard_map/all_to_all | solution.py:150
  340.5 2.5 gather_fusion.1
  345.2 109.4 %all-to-all-done.1 = bf16[16,48,1536]{2,1,0:T(8,128)(2,1)S(1)} async-done(((bf16[16,48,1536]{2,1,0:T(8,128)(2,1)}), bf16[16,48,1536]{2,1,0:T(8,128)(2,1)S(1)}, u32[]{:S(2)}, u32[]{:S(2)}) %all-to-all-start.1) | async-done | bytes 2359328 | tf_op jit(solution)/shard_map/all_to_all | solution.py:150
  454.6 10.4 %all-to-all-start.3 = ((bf16[16,2,4096]{2,1,0:T(2,128)(2,1)}), bf16[16,2,4096]{2,1,0:T(2,128)(2,1)S(1)}, u32[]{:S(2)}, u32[]{:S(2)}) async-start(bf16[16,2,4096]{2,1,0:T(2,128)(2,1)} %reshape.219), calls=%async_computation.3 | async-start | bytes 524288 | tf_op jit(solution)/shard_map/all_to_all | solution.py:101
  465.0 2.8 fusion.40
  467.8 5.3 convolution_convert_fusion
  473.1 85.0 %all-to-all-done.3 = bf16[16,2,4096]{2,1,0:T(2,128)(2,1)S(1)} async-done(((bf16[16,2,4096]{2,1,0:T(2,128)(2,1)}), bf16[16,2,4096]{2,1,0:T(2,128)(2,1)S(1)}, u32[]{:S(2)}, u32[]{:S(2)}) %all-to-all-start.3) | async-done | bytes 262176 | tf_op jit(solution)/shard_map/all_to_all | solution.py:101
  558.1 4.5 all-to-all-start.2
  564.1 2.2 copy.53
  566.3 2.1 all_to_all.42
  568.5 33.7 %all-to-all-done.2 = bf16[16,48,1536]{2,1,0:T(8,128)(2,1)S(1)} async-done(((bf16[16,48,1536]{2,1,0:T(8,128)(2,1)}), bf16[16,48,1536]{2,1,0:T(8,128)(2,1)S(1)}, u32[]{:S(2)}, u32[]{:S(2)}) %all-to-all-start.2) | async-done | bytes 2359328 | tf_op jit(solution)/shard_map/all_to_all | solution.py:158
  605.5 2.3 gather_fusion
  607.9 2.3 reshape.198
  610.2 2.2 multiply_reduce_fusion
  (104 shorter events, 38.4 us)
Async XLA Ops:
  7.2 460.7 %copy-start = (bf16[256,1536]{1,0:T(8,128)(2,1)S(1)}, bf16[256,1536]{1,0:T(8,128)(2,1)}, u32[]{:S(2)}) copy-start(bf16[256,1536]{1,0:T(8,128)(2,1)} %param.26) | copy-start | bytes 2359300
  7.2 155.8 %all-gather.4.cloned.1.call-start = ((), (), s32[]{:S(2)}) async-start(), calls=%async_computation.4 | async-start | bytes 6684672 | tf_op jit(solution)/shard_map/all_gather | solution.py:87
  10.4 159.5 %copy-start.8 = (s32[128]{0:T(128)S(1)}, s32[128]{0:T(128)}, u32[]{:S(2)}) copy-start(s32[128]{0:T(128)} %param.21) | copy-start | bytes 1540
  10.4 316.8 %all-gather.6.cloned.1.call-start = ((), (), s32[]{:S(2)}) async-start(), calls=%async_computation.5 | async-start | bytes 3342336 | tf_op jit(solution)/shard_map/all_gather | solution.py:121
  167.9 47.3 %collective-permute-start = (bf16[2048,64]{0,1:T(8,128)(2,1)S(1)}, bf16[2048,64]{0,1:T(8,128)(2,1)S(1)}, u32[]{:S(2)}, u32[]{:S(2)}) collective-permute-start(bf16[2048,64]{0,1:T(8,128)(2,1)S(1)} %slice.28), channel_id=1, source_target_pairs={{0,8},{8,0},{1,9},{9,1},{2,10},{10,2},{3,11},{11,3},{4,12},{12,4},... | collective-permute-start | bytes 786440 | tf_op jit(solution)/shard_map/ppermute | solution.py:17
  213.2 7.0 %collective-permute-start.2 = (s32[2048]{0:T(1024)S(1)}, s32[2048]{0:T(1024)S(1)}, u32[]{:S(2)}, u32[]{:S(2)}) collective-permute-start(s32[2048]{0:T(1024)S(1)} %bitcast.97), channel_id=1, source_target_pairs={{0,16},{16,32},{32,48},{48,64},{64,80},{80,96},{96,112},{112,128},... | collective-permute-start | bytes 24584 | tf_op jit(solution)/shard_map/ppermute | solution.py:23
  215.3 12.4 %collective-permute-start.3 = (bf16[2048,64]{0,1:T(8,128)(2,1)S(1)}, bf16[2048,64]{0,1:T(8,128)(2,1)S(1)}, u32[]{:S(2)}, u32[]{:S(2)}) collective-permute-start(bf16[2048,64]{0,1:T(8,128)(2,1)S(1)} %get-tuple-element.131), channel_id=1, source_target_pairs={{0,16},{16,32},{32,48},{48,64},{64,80},{80,96},{96,112},{112,128},... | collective-permute-start | bytes 786440 | tf_op jit(solution)/shard_map/ppermute | solution.py:23
  220.2 13.1 %collective-permute-start.1 = (bf16[2048,64]{0,1:T(8,128)(2,1)S(1)}, bf16[2048,64]{0,1:T(8,128)(2,1)S(1)}, u32[]{:S(2)}, u32[]{:S(2)}) collective-permute-start(bf16[2048,64]{0,1:T(8,128)(2,1)S(1)} %get-tuple-element.132), channel_id=1, source_target_pairs={{0,16},{16,32},{32,48},{48,64},{64,80},{80,96},{96,112},{112,128},... | collective-permute-start | bytes 786440 | tf_op jit(solution)/shard_map/ppermute | solution.py:23
  233.3 36.9 %copy-start.6 = (s32[128,2]{0,1:T(2,128)S(1)}, s32[128,2]{0,1:T(2,128)}, u32[]{:S(2)}) copy-start(s32[128,2]{0,1:T(2,128)} %param.22) | copy-start | bytes 3076
  248.8 78.4 %copy-start.4 = (bf16[128,1536]{1,0:T(8,128)(2,1)S(1)}, bf16[128,1536]{1,0:T(8,128)(2,1)}, u32[]{:S(2)}) copy-start(bf16[128,1536]{1,0:T(8,128)(2,1)} %param.15) | copy-start | bytes 1179652
  249.9 77.3 %all-to-all-start = ((bf16[16,128,64]{1,2,0:T(8,128)(2,1)}), bf16[16,128,64]{1,2,0:T(8,128)(2,1)S(1)}, u32[]{:S(2)}, u32[]{:S(2)}) async-start(bf16[16,128,64]{1,2,0:T(8,128)(2,1)} %copy.44), calls=%async_computation | async-start | bytes 524288 | tf_op jit(solution)/shard_map/all_to_all | solution.py:118
  271.8 58.9 %copy-start.5 = (f32[1536]{0:T(1024)S(1)}, f32[1536]{0:T(1024)}, u32[]{:S(2)}) copy-start(f32[1536]{0:T(1024)} %param.17) | copy-start | bytes 18436
  329.8 0.9 copy-start.2
  332.9 6.5 %copy-start.9 = (s32[1,128]{1,0:T(1,128)S(1)}, s32[1,128]{1,0:T(1,128)}, u32[]{:S(2)}) copy-start(s32[1,128]{1,0:T(1,128)} %param.27) | copy-start | bytes 1540
  332.9 121.7 %all-to-all-start.1 = ((bf16[16,48,1536]{2,1,0:T(8,128)(2,1)}), bf16[16,48,1536]{2,1,0:T(8,128)(2,1)S(1)}, u32[]{:S(2)}, u32[]{:S(2)}) async-start(bf16[16,48,1536]{2,1,0:T(8,128)(2,1)} %bitcast.17), calls=%async_computation.1 | async-start | bytes 4718592 | tf_op jit(solution)/shard_map/all_to_all | solution.py:150
  454.6 103.5 %all-to-all-start.3 = ((bf16[16,2,4096]{2,1,0:T(2,128)(2,1)}), bf16[16,2,4096]{2,1,0:T(2,128)(2,1)S(1)}, u32[]{:S(2)}, u32[]{:S(2)}) async-start(bf16[16,2,4096]{2,1,0:T(2,128)(2,1)} %reshape.219), calls=%async_computation.3 | async-start | bytes 524288 | tf_op jit(solution)/shard_map/all_to_all | solution.py:101
  558.1 4.7 copy-start.7
  558.1 44.0 %all-to-all-start.2 = ((bf16[16,48,1536]{2,1,0:T(8,128)(2,1)}), bf16[16,48,1536]{2,1,0:T(8,128)(2,1)S(1)}, u32[]{:S(2)}, u32[]{:S(2)}) async-start(bf16[16,48,1536]{2,1,0:T(8,128)(2,1)} %bitcast.93), calls=%async_computation.2 | async-start | bytes 4718592 | tf_op jit(solution)/shard_map/all_to_all | solution.py:158
  602.2 1.4 copy-start.1
  607.9 4.5 copy-start.3
Sparse Core Ops, SparseCore 0:
  11.9 151.0 all-gather.3
  215.3 111.8 all-gather.5
where the time goes:
time: 621 us; the launch traced here: 620 us
  waiting for transfers between devices  450 us (72%)
  starting transfers between devices  49.5 us (8%)
  blocking collectives  43.4 us (7%)
  local copies, waits for them, and re-layouts  24.9 us (4%)
  matrix products  23.5 us (4%)
  between operations  14.4 us (2%)
  other arithmetic  11.5 us (2%)
    all_gather x1, waiting for transfers between devices, body(): lax.all_gather(normed_in, 'tp', axis=0, tiled=True)  153 us
    all_to_all x1, waiting for transfers between devices, body(): lax.all_to_all(send_buf, 'tp', split_axis=0, concat_axis=0, tiled=True)  109 us
    all_to_all x1, waiting for transfers between devices, body(): lax.all_to_all(ordered_pages, 'tp', split_axis=0, concat_axis=2, tiled=True)  85 us
    all_gather x1, waiting for transfers between devices, body(): lax.all_gather(w_out, 'tp', axis=0, tiled=True)  55.3 us
    all_gather x1, blocking collectives, body(): seg_all = lax.all_gather(segment_ids, 'tp', axis=0, tiled=True)  43.4 us
    all_to_all x1, waiting for transfers between devices, body(): lax.all_to_all(half_out, 'tp', split_axis=0, concat_axis=0, tiled=True)  33.7 us
    all_to_all x1, starting transfers between devices, body(): lax.all_to_all(attended, 'tp', split_axis=0, concat_axis=1, tiled=True)  20.4 us
    ppermute x3, waiting for transfers between devices, from_behind(): return lax.ppermute(block, axis, route)  14.1 us
  transfers between devices with their start and end apart: 10, of which 8 were waited for; matrix products, arithmetic and copies ran while one was open for 5% of the time, Pallas kernels for 0%

commit v1 on v0

--- a/solution.py
+++ b/solution.py
@@ -84,7 +84,9 @@
     normed_in = rms_scale(tokens, attn_gain)
     both_cols = jnp.concatenate([w_query, key_value_weight], axis=1)
     projected = jnp.dot(
-        lax.all_gather(normed_in, "tp", axis=0, tiled=True),
+        jnp.concatenate(
+            lax.all_to_all(jnp.stack([normed_in] * lax.axis_size("tp")), "tp", 0, 0), axis=0
+        ),
         both_cols,
         preferred_element_type=jnp.float32,
     ).astype(jnp.bfloat16)

time: 621 us -> 748 us (1.20)
  the two profiles are of different devices: /device:TPU:103 before, /device:TPU:207 now
where the time goes in v1:
time: 748 us; the launch traced here: 747 us
  blocking collectives  330 us (44%)
  waiting for transfers between devices  293 us (39%)
  starting transfers between devices  49.4 us (7%)
  local copies, waits for them, and re-layouts  25.5 us (3%)
  matrix products  20.7 us (3%)
  between operations  14.4 us (2%)
  other arithmetic  10.8 us (1%)
    all_to_all x1, blocking collectives, body(): lax.all_to_all(jnp.stack([normed_in] * lax.axis_size('tp')), 'tp', 0, 0)  296 us
    all_to_all x1, waiting for transfers between devices, body(): lax.all_to_all(send_buf, 'tp', split_axis=0, concat_axis=0, tiled=True)  118 us
    all_to_all x1, waiting for transfers between devices, body(): lax.all_to_all(half_out, 'tp', split_axis=0, concat_axis=0, tiled=True)  95.6 us
    all_gather x1, waiting for transfers between devices, body(): lax.all_gather(w_out, 'tp', axis=0, tiled=True)  55.2 us
    all_gather x1, blocking collectives, body(): seg_all = lax.all_gather(segment_ids, 'tp', axis=0, tiled=True)  33.7 us
    ppermute x3, waiting for transfers between devices, from_behind(): return lax.ppermute(block, axis, route)  16.7 us
    all_to_all x1, starting transfers between devices, body(): lax.all_to_all(attended, 'tp', split_axis=0, concat_axis=1, tiled=True)  15.9 us
  transfers between devices with their start and end apart: 9, of which 7 were waited for; matrix products, arithmetic and copies ran while one was open for 4% of the time, Pallas kernels for 0%

profile of v1, /device:TPU:207, one launch (start us, length us, event | category | flops | bytes accessed | tf_op | source)
XLA Modules:
  0.0 746.6 jit_solution(5129356998474854661)
XLA Ops:
  10.3 296.4 %all_to_all.52 = bf16[16,128,1536]{2,1,0:T(8,128)(2,1)S(1)} all-to-all(bf16[16,128,1536]{2,1,0:T(8,128)(2,1)S(1)} %stack.2), channel_id=1, replica_groups=mesh['grp'=32,'tp'=16] {'tp'}, dimensions={0} | all-to-all | bytes 12582912 | tf_op jit(solution)/shard_map/all_to_all | solution.py:88
  308.8 3.3 collective-permute-start
  312.1 33.7 %all-gather = s32[16,1,128]{2,1,0:T(1,128)S(1)} all-gather(s32[1,1,128]{2,1,0:T(1,128)S(1)} %bitcast.104), channel_id=1, replica_groups=mesh['grp'=32,'tp'=16] {'tp'}, dimensions={0}, use_global_device_ids=true | all-gather | bytes 8704 | tf_op jit(solution)/shard_map/all_gather | solution.py:104
  345.8 6.2 collective-permute-start.2
  354.0 7.4 collective-permute-done.2
  361.4 3.7 collective-permute-start.1
  365.1 3.8 collective-permute-done.3
  368.9 5.6 collective-permute-done.1
  374.6 15.4 %while.12 = (s32[]{:T(128)}, bf16[4,512,1,64]{1,3,2,0:T(8,128)(2,1)S(1)}, s32[4]{0:T(128)S(1)}, bf16[4096,1,64]{0,2,1:T(8,128)(2,1)S(1)}, s32[2048]{0:T(1024)S(1...) while((s32[]{:T(128)}, ...), condition=%wide.region_4.5_spmd, body=%wide.region_1.4_spmd.sunk | while | flops 210011136 | bytes 10017057 | solution.py:61
  391.1 15.9 %all-to-all-start.1 = ((bf16[16,128,64]{1,2,0:T(8,128)(2,1)}), bf16[16,128,64]{1,2,0:T(8,128)(2,1)S(1)}, u32[]{:S(2)}, u32[]{:S(2)}) async-start(bf16[16,128,64]{1,2,0:T(8,128)(2,1)} %copy.44), calls=%async_computation.1 | async-start | bytes 524288 | tf_op jit(solution)/shard_map/all_to_all | solution.py:120
  408.6 55.2 %all-gather.3.cloned.1.call-done = bf16[1024,1536]{1,0:T(8,128)(2,1)} async-done(((bf16[64,1536]{1,0:T(8,128)(2,1)}), bf16[1024,1536]{1,0:T(8,128)(2,1)}) %all-gather.3.cloned.1.call-update) | async-done | bytes 3145744 | tf_op jit(solution)/shard_map/all_gather | solution.py:123
  463.9 2.6 multiply_reduce_fusion.1
  469.5 4.6 all-to-all-start.2
  475.2 2.5 gather_fusion.1
  479.9 118.4 %all-to-all-done.2 = bf16[16,48,1536]{2,1,0:T(8,128)(2,1)S(1)} async-done(((bf16[16,48,1536]{2,1,0:T(8,128)(2,1)}), bf16[16,48,1536]{2,1,0:T(8,128)(2,1)S(1)}, u32[]{:S(2)}, u32[]{:S(2)}) %all-to-all-start.2) | async-done | bytes 2359328 | tf_op jit(solution)/shard_map/all_to_all | solution.py:152
  598.4 6.3 all-to-all-start.4
  604.7 2.8 fusion.40
  607.5 5.3 convolution_convert_fusion
  612.8 7.0 all-to-all-done.4
  619.7 7.6 %all-to-all-start.3 = ((bf16[16,48,1536]{2,1,0:T(8,128)(2,1)}), bf16[16,48,1536]{2,1,0:T(8,128)(2,1)S(1)}, u32[]{:S(2)}, u32[]{:S(2)}) async-start(bf16[16,48,1536]{2,1,0:T(8,128)(2,1)} %bitcast.95), calls=%async_computation.3 | async-start | bytes 4718592 | tf_op jit(solution)/shard_map/all_to_all | solution.py:160
  628.8 2.2 copy.53
  633.1 95.6 %all-to-all-done.3 = bf16[16,48,1536]{2,1,0:T(8,128)(2,1)S(1)} async-done(((bf16[16,48,1536]{2,1,0:T(8,128)(2,1)}), bf16[16,48,1536]{2,1,0:T(8,128)(2,1)S(1)}, u32[]{:S(2)}, u32[]{:S(2)}) %all-to-all-start.3) | async-done | bytes 2359328 | tf_op jit(solution)/shard_map/all_to_all | solution.py:160
  732.1 2.3 gather_fusion
  734.5 2.3 reshape.204
  (107 shorter events, 38.9 us)
Async XLA Ops:
  7.2 600.3 %copy-start = (bf16[256,1536]{1,0:T(8,128)(2,1)S(1)}, bf16[256,1536]{1,0:T(8,128)(2,1)}, u32[]{:S(2)}) copy-start(bf16[256,1536]{1,0:T(8,128)(2,1)} %param.26) | copy-start | bytes 2359300
  7.2 456.7 %all-gather.3.cloned.1.call-start = ((), (), s32[]{:S(2)}) async-start(), calls=%async_computation.5 | async-start | bytes 3342336 | tf_op jit(solution)/shard_map/all_gather | solution.py:123
  10.2 296.4 %copy-start.9 = (bf16[1536,64]{0,1:T(8,128)(2,1)S(1)}, bf16[1536,64]{0,1:T(8,128)(2,1)}, u32[]{:S(2)}) copy-start(bf16[1536,64]{0,1:T(8,128)(2,1)} %param.19) | copy-start | bytes 589828
  10.2 296.4 %copy-start.10 = (bf16[1536,64]{0,1:T(8,128)(2,1)S(1)}, bf16[1536,64]{0,1:T(8,128)(2,1)}, u32[]{:S(2)}) copy-start(bf16[1536,64]{0,1:T(8,128)(2,1)} %param.18) | copy-start | bytes 589828
  306.6 5.4 copy-start.8
  308.8 43.3 %collective-permute-start = (bf16[2048,64]{0,1:T(8,128)(2,1)S(1)}, bf16[2048,64]{0,1:T(8,128)(2,1)S(1)}, u32[]{:S(2)}, u32[]{:S(2)}) collective-permute-start(bf16[2048,64]{0,1:T(8,128)(2,1)S(1)} %slice.28), channel_id=1, source_target_pairs={{0,8},{8,0},{1,9},{9,1},{2,10},{10,2},{3,11},{11,3},{4,12},{12,4},... | collective-permute-start | bytes 786440 | tf_op jit(solution)/shard_map/ppermute | solution.py:17
  345.8 15.6 %collective-permute-start.2 = (s32[2048]{0:T(1024)S(1)}, s32[2048]{0:T(1024)S(1)}, u32[]{:S(2)}, u32[]{:S(2)}) collective-permute-start(s32[2048]{0:T(1024)S(1)} %bitcast.99), channel_id=1, source_target_pairs={{0,16},{16,32},{32,48},{48,64},{64,80},{80,96},{96,112},{112,128},... | collective-permute-start | bytes 24584 | tf_op jit(solution)/shard_map/ppermute | solution.py:23
  352.1 16.8 %collective-permute-start.3 = (bf16[2048,64]{0,1:T(8,128)(2,1)S(1)}, bf16[2048,64]{0,1:T(8,128)(2,1)S(1)}, u32[]{:S(2)}, u32[]{:S(2)}) collective-permute-start(bf16[2048,64]{0,1:T(8,128)(2,1)S(1)} %get-tuple-element.131), channel_id=1, source_target_pairs={{0,16},{16,32},{32,48},{48,64},{64,80},{80,96},{96,112},{112,128},... | collective-permute-start | bytes 786440 | tf_op jit(solution)/shard_map/ppermute | solution.py:23
  361.4 13.1 %collective-permute-start.1 = (bf16[2048,64]{0,1:T(8,128)(2,1)S(1)}, bf16[2048,64]{0,1:T(8,128)(2,1)S(1)}, u32[]{:S(2)}, u32[]{:S(2)}) collective-permute-start(bf16[2048,64]{0,1:T(8,128)(2,1)S(1)} %get-tuple-element.132), channel_id=1, source_target_pairs={{0,16},{16,32},{32,48},{48,64},{64,80},{80,96},{96,112},{112,128},... | collective-permute-start | bytes 786440 | tf_op jit(solution)/shard_map/ppermute | solution.py:23
  374.5 32.4 %copy-start.6 = (s32[128,2]{0,1:T(2,128)S(1)}, s32[128,2]{0,1:T(2,128)}, u32[]{:S(2)}) copy-start(s32[128,2]{0,1:T(2,128)} %param.22) | copy-start | bytes 3076
  390.0 73.9 %copy-start.4 = (bf16[128,1536]{1,0:T(8,128)(2,1)S(1)}, bf16[128,1536]{1,0:T(8,128)(2,1)}, u32[]{:S(2)}) copy-start(bf16[128,1536]{1,0:T(8,128)(2,1)} %param.15) | copy-start | bytes 1179652
  391.1 72.8 %all-to-all-start.1 = ((bf16[16,128,64]{1,2,0:T(8,128)(2,1)}), bf16[16,128,64]{1,2,0:T(8,128)(2,1)S(1)}, u32[]{:S(2)}, u32[]{:S(2)}) async-start(bf16[16,128,64]{1,2,0:T(8,128)(2,1)} %copy.44), calls=%async_computation.1 | async-start | bytes 524288 | tf_op jit(solution)/shard_map/all_to_all | solution.py:120
  408.5 58.8 %copy-start.5 = (f32[1536]{0:T(1024)S(1)}, f32[1536]{0:T(1024)}, u32[]{:S(2)}) copy-start(f32[1536]{0:T(1024)} %param.17) | copy-start | bytes 18436
  466.4 0.9 copy-start.2
  469.5 4.6 copy-start.11
  469.5 128.8 %all-to-all-start.2 = ((bf16[16,48,1536]{2,1,0:T(8,128)(2,1)}), bf16[16,48,1536]{2,1,0:T(8,128)(2,1)S(1)}, u32[]{:S(2)}, u32[]{:S(2)}) async-start(bf16[16,48,1536]{2,1,0:T(8,128)(2,1)} %bitcast.18), calls=%async_computation.2 | async-start | bytes 4718592 | tf_op jit(solution)/shard_map/all_to_all | solution.py:152
  598.4 21.4 %all-to-all-start.4 = ((bf16[16,2,4096]{2,1,0:T(2,128)(2,1)}), bf16[16,2,4096]{2,1,0:T(2,128)(2,1)S(1)}, u32[]{:S(2)}, u32[]{:S(2)}) async-start(bf16[16,2,4096]{2,1,0:T(2,128)(2,1)} %reshape.225), calls=%async_computation.4 | async-start | bytes 524288 | tf_op jit(solution)/shard_map/all_to_all | solution.py:103
  619.7 7.7 %copy-start.7 = (f32[128,2]{0,1:T(2,128)S(1)}, f32[128,2]{0,1:T(2,128)}, u32[]{:S(2)}) copy-start(f32[128,2]{0,1:T(2,128)} %param.23) | copy-start | bytes 3076
  619.7 109.0 %all-to-all-start.3 = ((bf16[16,48,1536]{2,1,0:T(8,128)(2,1)}), bf16[16,48,1536]{2,1,0:T(8,128)(2,1)S(1)}, u32[]{:S(2)}, u32[]{:S(2)}) async-start(bf16[16,48,1536]{2,1,0:T(8,128)(2,1)} %bitcast.95), calls=%async_computation.3 | async-start | bytes 4718592 | tf_op jit(solution)/shard_map/all_to_all | solution.py:160
  728.7 1.4 copy-start.1
  734.4 4.5 copy-start.3
Sparse Core Ops, SparseCore 0:
  352.1 111.6 all-gather.2
